TPU v7x, 32 devices: a whole 2x2x4 slice. The times are simulated.
32 devices in a mesh: leaf: 8 (over y, x, core), loop: 4 (over z).
Axes of the slice: x: 2, y: 2, z: 4, core: 2. Of those that a mesh axis runs over, the one named last changes fastest.
Arguments:
- jacobian_t: bfloat16 [4, 8192, 512], P('loop', 'leaf'), may hold values from -6 to 6
- leaf_block: bfloat16 [4, 8192, 1024], P('loop', 'leaf'), may hold values from -0.1875 to 0.1875
- left_basis: bfloat16 [4, 8192, 128], P('loop', 'leaf'), may hold values from -0.5 to 0.5
- right_basis: bfloat16 [4, 8192, 128], P('loop', 'leaf'), may hold values from -0.1875 to 0.1875
- couplings: bfloat16 [4, 24, 128, 128], P('loop', 'leaf'), may hold values from -0.5 to 0.5
- group_coupling: bfloat16 [4, 16, 128, 128], P('loop', 'leaf'), may hold values from -0.5 to 0.5
- obs_order: int32 [512], replicated, may hold values from 0 to 511, each once
Outputs:
- cross_cov: bfloat16 [4, 8192, 512], P('loop', 'leaf')
- projected: float32 [512, 512], P('leaf')
Inputs may be any that keep to these rules, and one draw needn't show every extreme that they name: `obs_order`: each observation 0 to 511 appears exactly once.
All inputs are finite; a program needn't handle non-finite values.
Results may differ from a plain program's by a relative error of at most 0.005.
Values sent between devices are 32-bit elements; how exact they have to be, the bound alone decides.
A program may use at most 64 MiB of HBM per device.

v0:
```python
import jax
import jax.numpy as jnp
from jax import lax
from jax.sharding import PartitionSpec as P


def partner(value, axis, stride):
    mask = 2**stride
    pairs = [(source, source ^ mask) for source in range(lax.axis_size(axis))]
    return lax.ppermute(value, axis, pairs)


def from_behind(shard, axis, by):
    devices = lax.axis_size(axis)
    return lax.ppermute(shard, axis, [(i, (i + by) % devices) for i in range(devices)])


def body(jacobian_t, leaf_block, left_basis, right_basis, couplings, group_coupling, obs_order):
    highest = lax.Precision.HIGHEST
    field = jacobian_t[0]
    block = leaf_block[0]
    lefts = left_basis[0]
    rights = right_basis[0]
    coupled = couplings[0].astype(jnp.float32)
    neighbour = group_coupling[0].astype(jnp.float32)
    coef = lax.dot_general(
        rights, field, (((0,), (0,)), ((), ())), preferred_element_type=jnp.float32
    )
    levels = lax.axis_size("leaf").bit_length() - 1
    total = coef
    mixed = jnp.zeros_like(coef)
    for level in range(levels):
        other = partner(total, "leaf", level)
        mixed = mixed + jnp.dot(coupled[level], other, precision=highest)
        total = total + other
    before = from_behind(total, "loop", 1)
    after = from_behind(total, "loop", -1)
    mixed = mixed + jnp.dot(neighbour[0], before, precision=highest)
    mixed = mixed + jnp.dot(neighbour[1], after, precision=highest)
    mixed = mixed.astype(jnp.bfloat16)
    near = jnp.dot(block, field, preferred_element_type=jnp.float32)
    far = jnp.dot(lefts, mixed, preferred_element_type=jnp.float32)
    cross = (near + far).astype(jnp.bfloat16)
    partial_value = lax.dot_general(
        field, cross, (((0,), (0,)), ((), ())), preferred_element_type=jnp.float32
    )
    ordered = partial_value[obs_order]
    mine = lax.psum_scatter(ordered, "leaf", scatter_dimension=0, tiled=True)
    projected = lax.psum(mine, "loop")
    return (cross[None], projected)


def solution(mesh):
    in_specs = (
        P("loop", "leaf", None),
        P("loop", "leaf", None),
        P("loop", "leaf", None),
        P("loop", "leaf", None),
        P("loop", "leaf", None, None),
        P("loop", "leaf", None, None),
        P(),
    )
    out_specs = (P("loop", "leaf", None), P("leaf", None))
    return jax.shard_map(body, mesh=mesh, in_specs=in_specs, out_specs=out_specs, check_vma=False)
```

profile of v0, /device:TPU:0, one launch (start us, length us, event | category | flops | bytes accessed | tf_op | source)
XLA Modules:
  0.0 131.8 jit_solution(6118895068990609260)
XLA Ops:
  7.2 0.0 copy-start
  7.2 0.0 copy-start.2
  7.2 0.0 copy-start.6
  7.2 0.0 reduce-scatter.2.cloned.1.call-start
  7.2 1.8 %fusion.8 = f32[128,512]{1,0:T(8,128)S(1)} fusion(bf16[1,1024,512]{2,1,0:T(8,128)(2,1)} %param.7, bf16[1,1024,128]{2,1,0:T(8,128)(2,1)} %param.10), kind=kOutput, calls=%fused_computation.12 | convolution fusion | flops 134217728 | bytes 1572864 | tf_op jit(solution)/shard_map/dot_general | solution.py:26
  9.0 0.6 collective-permute-start
  9.6 1.2 collective-permute-done
  10.8 2.9 %collective-permute-start.1 = (f32[128,512]{1,0:T(8,128)S(1)}, f32[128,512]{1,0:T(8,128)S(1)}, u32[]{:S(2)}, u32[]{:S(2)}) collective-permute-start(f32[128,512]{1,0:T(8,128)S(1)} %add.40), channel_id=1, source_target_pairs={{0,8},{4,12},{8,0},{12,4},{16,24},{20,28},{24,16},{28,20},{1,9},{5... | collective-permute-start | bytes 786440 | tf_op jit(solution)/shard_map/ppermute | solution.py:10
  13.7 0.0 copy-done.6
  13.7 6.6 %collective-permute-done.1 = f32[128,512]{1,0:T(8,128)S(1)} collective-permute-done((f32[128,512]{1,0:T(8,128)S(1)}, f32[128,512]{1,0:T(8,128)S(1)}, u32[]{:S(2)}, u32[]{:S(2)}) %collective-permute-start.1) | collective-permute-done | bytes 262176 | tf_op jit(solution)/shard_map/ppermute | solution.py:10
  20.4 0.0 copy-start.4
  20.4 0.0 copy-start.5
  20.4 1.8 %collective-permute-start.2 = (f32[128,512]{1,0:T(8,128)S(1)}, f32[128,512]{1,0:T(8,128)S(1)}, u32[]{:S(2)}, u32[]{:S(2)}) collective-permute-start(f32[128,512]{1,0:T(8,128)S(1)} %add.42), channel_id=1, source_target_pairs={{0,16},{4,20},{8,24},{12,28},{16,0},{20,4},{24,8},{28,12},{1,17},{... | collective-permute-start | bytes 786440 | tf_op jit(solution)/shard_map/ppermute | solution.py:10
  22.2 0.0 copy-done
  22.2 0.0 copy-done.2
  22.2 1.2 fusion.1
  23.5 0.0 copy-start.3
  23.5 4.7 %collective-permute-done.2 = f32[128,512]{1,0:T(8,128)S(1)} collective-permute-done((f32[128,512]{1,0:T(8,128)S(1)}, f32[128,512]{1,0:T(8,128)S(1)}, u32[]{:S(2)}, u32[]{:S(2)}) %collective-permute-start.2) | collective-permute-done | bytes 262176 | tf_op jit(solution)/shard_map/ppermute | solution.py:10
  28.3 3.6 %collective-permute-start.4 = (f32[128,512]{1,0:T(8,128)S(1)}, f32[128,512]{1,0:T(8,128)S(1)}, u32[]{:S(2)}, u32[]{:S(2)}) collective-permute-start(f32[128,512]{1,0:T(8,128)S(1)} %add.44), channel_id=1, source_target_pairs={{0,3},{1,0},{2,1},{3,2},{4,7},{5,4},{6,5},{7,6},{8,11},{9,8},{10,9... | collective-permute-start | bytes 786440 | tf_op jit(solution)/shard_map/ppermute | solution.py:15
  31.9 0.0 copy-done.4
  31.9 0.4 fusion.19
  32.3 0.1 collective-permute-start.3
  32.4 0.4 fusion.17
  32.7 5.8 %collective-permute-done.4 = f32[128,512]{1,0:T(8,128)S(1)} collective-permute-done((f32[128,512]{1,0:T(8,128)S(1)}, f32[128,512]{1,0:T(8,128)S(1)}, u32[]{:S(2)}, u32[]{:S(2)}) %collective-permute-start.4) | collective-permute-done | bytes 262176 | tf_op jit(solution)/shard_map/ppermute | solution.py:15
  38.6 0.0 copy-done.5
  38.6 0.4 fusion.13
  39.0 3.6 %collective-permute-done.3 = f32[128,512]{1,0:T(8,128)S(1)} collective-permute-done((f32[128,512]{1,0:T(8,128)S(1)}, f32[128,512]{1,0:T(8,128)S(1)}, u32[]{:S(2)}, u32[]{:S(2)}) %collective-permute-start.3) | collective-permute-done | bytes 262176 | tf_op jit(solution)/shard_map/ppermute | solution.py:15
  42.6 0.4 fusion.15
  43.0 0.4 fusion.6
  43.4 0.0 copy-done.3
  43.4 0.4 fusion
  43.8 0.0 copy-start.1
  43.8 1.0 copy-done.1
  44.8 1.7 %convolution_bitcast_fusion = f32[512,512]{0,1:T(8,128)} fusion(bf16[1024,512]{1,0:T(8,128)(2,1)S(1)} %fusion, bf16[1,1024,512]{2,1,0:T(8,128)(2,1)S(1)} %copy-done.2), kind=kOutput, calls=%fused_computation.5 | convolution fusion | flops 536870912 | bytes 3145728 | tf_op jit(solution)/shard_map/dot_general | solution.py:44
  46.5 1.6 %copy.10 = f32[512,512]{1,0:T(8,128)S(1)} copy(f32[512,512]{0,1:T(8,128)} %convolution_bitcast_fusion) | data formatting | bytes 2097152 | tf_op jit(solution)/shard_map/dot_general | solution.py:44
  48.1 2.3 %gather_fusion = f32[512,512]{1,0:T(8,128)} fusion(f32[512,512]{1,0:T(8,128)S(1)} %copy.10, s32[1024]{0:T(1024)S(1)} %pad_clamp_fusion), kind=kCustom, calls=%fused_computation | custom fusion | bytes 2099200 | tf_op jit(solution)/shard_map/gather | solution.py:47
  50.4 0.0 reduce-scatter.2.cloned.1.call-update
  50.4 0.0 all-reduce.2.cloned.1.call-start
  50.5 35.9 %reduce-scatter.2.cloned.1.call-done = f32[64,512]{1,0:T(8,128)} async-done(((f32[512,512]{1,0:T(8,128)}), f32[64,512]{1,0:T(8,128)}) %reduce-scatter.2.cloned.1.call-update) | async-done | bytes 131088 | tf_op jit(solution)/shard_map/reduce_scatter | solution.py:48
  86.4 0.0 all-reduce.2.cloned.1.call-update
  86.4 37.0 %all-reduce.2.cloned.1.call-done = f32[64,512]{1,0:T(8,128)} async-done(((f32[64,512]{1,0:T(8,128)}), f32[64,512]{1,0:T(8,128)}) %all-reduce.2.cloned.1.call-update) | async-done | bytes 131088 | tf_op jit(solution)/shard_map/psum | solution.py:49
  123.4 1.6 %copy.13 = f32[64,512]{1,0:T(8,128)} copy(f32[64,512]{1,0:T(8,128)} %all-reduce.2.cloned.1.call-done) | data formatting | bytes 262144
  (5 shorter events, 0.1 us)
Async XLA Ops:
  7.2 15.1 %copy-start = (bf16[1,1024,1024]{2,1,0:T(8,128)(2,1)S(1)}, bf16[1,1024,1024]{2,1,0:T(8,128)(2,1)}, u32[]{:S(2)}) copy-start(bf16[1,1024,1024]{2,1,0:T(8,128)(2,1)} %param.8) | copy-start | bytes 6291460
  7.2 15.0 %copy-start.2 = (bf16[1,1024,512]{2,1,0:T(8,128)(2,1)S(1)}, bf16[1,1024,512]{2,1,0:T(8,128)(2,1)}, u32[]{:S(2)}) copy-start(bf16[1,1024,512]{2,1,0:T(8,128)(2,1)} %param.7) | copy-start | bytes 3145732
  7.2 6.5 %copy-start.6 = (s32[512]{0:T(512)S(1)}, s32[512]{0:T(512)}, u32[]{:S(2)}) copy-start(s32[512]{0:T(512)} %param.13) | copy-start | bytes 6148
  7.2 79.2 %reduce-scatter.2.cloned.1.call-start = ((), (), s32[]{:S(2)}) async-start(), calls=%async_computation.1 | async-start | bytes 1179648 | tf_op jit(solution)/shard_map/reduce_scatter | solution.py:48
  9.0 1.7 %collective-permute-start = (f32[128,512]{1,0:T(8,128)S(1)}, f32[128,512]{1,0:T(8,128)S(1)}, u32[]{:S(2)}, u32[]{:S(2)}) collective-permute-start(f32[128,512]{1,0:T(8,128)S(1)} %fusion.8), channel_id=1, source_target_pairs={{0,4},{4,0},{8,12},{12,8},{16,20},{20,16},{24,28},{28,24},{1,5},{5... | collective-permute-start | bytes 786440 | tf_op jit(solution)/shard_map/ppermute | solution.py:10
  10.8 9.5 %collective-permute-start.1 = (f32[128,512]{1,0:T(8,128)S(1)}, f32[128,512]{1,0:T(8,128)S(1)}, u32[]{:S(2)}, u32[]{:S(2)}) collective-permute-start(f32[128,512]{1,0:T(8,128)S(1)} %add.40), channel_id=1, source_target_pairs={{0,8},{4,12},{8,0},{12,4},{16,24},{20,28},{24,16},{28,20},{1,9},{5... | collective-permute-start | bytes 786440 | tf_op jit(solution)/shard_map/ppermute | solution.py:10
  20.4 11.5 %copy-start.4 = (bf16[1,3,128,128]{3,2,1,0:T(8,128)(2,1)S(1)}, bf16[1,3,128,128]{3,2,1,0:T(8,128)(2,1)}, u32[]{:S(2)}) copy-start(bf16[1,3,128,128]{3,2,1,0:T(8,128)(2,1)} %param.11) | copy-start | bytes 294916
  20.4 18.2 %copy-start.5 = (bf16[1,2,128,128]{3,2,1,0:T(8,128)(2,1)S(1)}, bf16[1,2,128,128]{3,2,1,0:T(8,128)(2,1)}, u32[]{:S(2)}) copy-start(bf16[1,2,128,128]{3,2,1,0:T(8,128)(2,1)} %param.12) | copy-start | bytes 196612
  20.4 7.8 %collective-permute-start.2 = (f32[128,512]{1,0:T(8,128)S(1)}, f32[128,512]{1,0:T(8,128)S(1)}, u32[]{:S(2)}, u32[]{:S(2)}) collective-permute-start(f32[128,512]{1,0:T(8,128)S(1)} %add.42), channel_id=1, source_target_pairs={{0,16},{4,20},{8,24},{12,28},{16,0},{20,4},{24,8},{28,12},{1,17},{... | collective-permute-start | bytes 786440 | tf_op jit(solution)/shard_map/ppermute | solution.py:10
  23.5 19.9 %copy-start.3 = (bf16[1,1024,128]{2,1,0:T(8,128)(2,1)S(1)}, bf16[1,1024,128]{2,1,0:T(8,128)(2,1)}, u32[]{:S(2)}) copy-start(bf16[1,1024,128]{2,1,0:T(8,128)(2,1)} %param.9) | copy-start | bytes 786436
  28.3 10.3 %collective-permute-start.4 = (f32[128,512]{1,0:T(8,128)S(1)}, f32[128,512]{1,0:T(8,128)S(1)}, u32[]{:S(2)}, u32[]{:S(2)}) collective-permute-start(f32[128,512]{1,0:T(8,128)S(1)} %add.44), channel_id=1, source_target_pairs={{0,3},{1,0},{2,1},{3,2},{4,7},{5,4},{6,5},{7,6},{8,11},{9,8},{10,9... | collective-permute-start | bytes 786440 | tf_op jit(solution)/shard_map/ppermute | solution.py:15
  32.3 10.3 %collective-permute-start.3 = (f32[128,512]{1,0:T(8,128)S(1)}, f32[128,512]{1,0:T(8,128)S(1)}, u32[]{:S(2)}, u32[]{:S(2)}) collective-permute-start(f32[128,512]{1,0:T(8,128)S(1)} %add.44), channel_id=1, source_target_pairs={{0,1},{1,2},{2,3},{3,0},{4,5},{5,6},{6,7},{7,4},{8,9},{9,10},{10,1... | collective-permute-start | bytes 786440 | tf_op jit(solution)/shard_map/ppermute | solution.py:15
  43.8 1.0 copy-start.1
  50.4 72.9 %all-reduce.2.cloned.1.call-start = ((), (), s32[]{:S(2)}) async-start(), calls=%async_computation.2 | async-start | bytes 262144 | tf_op jit(solution)/shard_map/psum | solution.py:49
Sparse Core Ops, SparseCore 0:
  50.5 35.7 reduce-scatter.1
  88.7 34.6 all-reduce.1
where the time goes:
time: 132 us
  waiting for transfers between devices  94.8 us (72%)
  between operations  14.2 us (11%)
  starting transfers between devices  9.07 us (7%)
  matrix products  7.13 us (5%)
  local copies, waits for them, and re-layouts  6.45 us (5%)
    psum x1, waiting for transfers between devices, body(): projected = lax.psum(mine, 'loop')  37 us
    reduce_scatter x1, waiting for transfers between devices, body(): mine = lax.psum_scatter(ordered, 'leaf', scatter_dimension=0, tiled=True)  35.9 us
    ppermute x3, waiting for transfers between devices, partner(): return lax.ppermute(value, axis, pairs)  12.5 us
    ppermute x2, waiting for transfers between devices, from_behind(): lax.ppermute(shard, axis, [(i, (i + by) % devices) for i in range(devices)])  9.41 us
    ppermute x3, starting transfers between devices, partner(): return lax.ppermute(value, axis, pairs)  5.31 us
    ppermute x2, starting transfers between devices, from_behind(): lax.ppermute(shard, axis, [(i, (i + by) % devices) for i in range(devices)])  3.68 us
  transfers between devices with their start and end apart: 7, of which 7 were waited for; matrix products, arithmetic and copies ran while one was open for 2% of the time, Pallas kernels for 0%

commit v1 on v0

v1 whole, which is shorter than its diff:
```python
import functools

import jax
import jax.numpy as jnp
from jax import lax
from jax.experimental import pallas as pl
from jax.experimental.pallas import tpu as pltpu
from jax.sharding import PartitionSpec as P

MESH = pl.DeviceIdType.MESH
F32 = jnp.float32
BF16 = jnp.bfloat16


def dot(a, b):
    return jnp.dot(a, b, preferred_element_type=F32)


def split(value):
    high = value.astype(BF16)
    low = (value - high.astype(F32)).astype(BF16)
    return high, low


def stacked(value):
    return jnp.concatenate(split(value), axis=0)


def doubled(value):
    return jnp.concatenate([value, value], axis=1)


def kernel(
    n_leaf, n_loop, x_hbm, l_hbm, u_hbm, v_hbm, c_hbm, g_hbm, order_ref,
    cross_hbm, proj_hbm,
    x_ref, l_ref, u_ref, v_ref, c_ref, xp_ref, m_ref, mb_ref, n_ref, nrecv_ref,
    coef_ref, sums_ref, sib_ref, tot_ref, ends_ref, csend_ref, crecv_ref,
    w_ref, wrecv_ref, mixsend_ref, mixrecv_ref, mixall_ref,
    f_ref, frecv_ref, zs_ref, zr_ref, red_ref, ag_ref, cross_ref, proj_ref,
    load_sem, store_sem, early_send, early_recv, chain_send, chain_recv,
    end_send, end_recv, mix_send, mix_recv, f_send, f_recv, z_send, z_recv,
    ag_send, ag_recv,
):
    levels = n_leaf.bit_length() - 1
    chips = n_leaf // 2
    chip_levels = levels - 1
    pieces, rank, width = sums_ref.shape[1:]
    cells, obs = x_ref.shape
    chip_rows = obs // chips
    z_rows = chip_rows // n_loop
    half_loop = n_loop // 2
    leaf = lax.axis_index("leaf")
    loop = lax.axis_index("loop")
    core = leaf % 2
    chip = leaf // 2
    sibling = leaf + 1 - 2 * core
    owner = loop // half_loop

    def partner(bit):
        mask = 2**bit
        return leaf + mask * (1 - 2 * ((leaf // mask) % 2))

    def tile_of(relative):
        index = 0
        for bit in range(chip_levels):
            step = 2**bit
            index = index + step * (((chip // step) + (relative // step) % 2) % 2)
        return index

    def send(src, dst, send_sem, recv_sem, to_leaf, to_loop):
        copy = pltpu.make_async_remote_copy(
            src_ref=src, dst_ref=dst, send_sem=send_sem, recv_sem=recv_sem,
            device_id={"leaf": to_leaf, "loop": to_loop}, device_id_type=MESH,
        )
        copy.start()
        return copy

    loads = []
    for number, (src, dst) in enumerate((
        (v_hbm.at[0], v_ref), (x_hbm.at[0], x_ref),
        (u_hbm.at[0], u_ref), (c_hbm.at[0], c_ref.at[pl.ds(0, levels)]),
        (g_hbm.at[0], c_ref.at[pl.ds(levels, 2)]), (l_hbm.at[0], l_ref),
    )):
        loads.append(pltpu.make_async_copy(src, dst, load_sem.at[number]))
        loads[-1].start()

    barrier = pltpu.get_barrier_semaphore()
    for bit in range(1, levels):
        pl.semaphore_signal(
            barrier, inc=1, device_id={"leaf": partner(bit), "loop": loop}, device_id_type=MESH
        )
    for offset in range(n_loop):
        there = (loop + offset) % n_loop
        for to_leaf in (leaf, sibling):
            if offset or to_leaf is sibling:
                pl.semaphore_signal(
                    barrier, inc=1, device_id={"leaf": to_leaf, "loop": there}, device_id_type=MESH
                )

    loads[0].wait()
    loads[1].wait()
    coef = lax.dot_general(
        v_ref[...], x_ref[...], (((0,), (0,)), ((), ())), preferred_element_type=F32
    )
    for part in range(2 * pieces):
        coef_ref[part] = coef[:, part * width:(part + 1) * width]
    pl.semaphore_wait(barrier, levels - 1 + 2 * n_loop - 1)
    mine, other = core * pieces, (1 - core) * pieces
    sent = []
    first = []
    for k in range(pieces):
        first.append(send(
            coef_ref.at[other + k], sib_ref.at[k], early_send.at[k], early_recv.at[k],
            sibling, loop,
        ))

    loads[3].wait()
    loads[4].wait()
    csend_ref[...] = c_ref[...].astype(F32)
    copy_c = send(
        csend_ref, crecv_ref, early_send.at[pieces], early_recv.at[pieces], sibling, loop
    )
    chain = {}
    for k in range(pieces):
        first[k].wait_recv()
        tot_ref[0, k] = coef_ref[mine + k] + sib_ref[k]
        chain[1, k] = send(
            tot_ref.at[0, k], sums_ref.at[0, k], chain_send.at[0, k], chain_recv.at[0, k],
            partner(1), loop,
        )

    onehot = (
        lax.broadcasted_iota(jnp.int32, (obs, obs), 0)
        == jnp.broadcast_to(order_ref[...], (obs, obs))
    ).astype(F32).astype(BF16)
    blocks = 4
    step = cells // blocks

    @pl.loop(0, blocks)
    def permute(i):
        rows = pl.ds(pl.multiple_of(i * step, step), step)
        xp_ref[rows, :] = dot(x_ref[rows, :], onehot).astype(BF16)

    loads[2].wait()
    w_ref[...] = lax.dot_general(
        xp_ref[...], u_ref[...], (((0,), (0,)), ((), ())), preferred_element_type=F32
    )
    copy_w = send(
        w_ref, wrecv_ref, early_send.at[pieces + 1], early_recv.at[pieces + 1], sibling, loop
    )
    loads[5].wait()

    def near():
        @pl.loop(0, blocks)
        def multiply(i):
            rows = pl.ds(pl.multiple_of(i * step, step), step)
            value = dot(l_ref[rows, :], x_ref[...])
            m_ref[rows, :] = value
            mb_ref[rows, :] = value.astype(BF16)

    def project():
        high = obs // blocks

        @pl.loop(0, blocks)
        def multiply(i):
            rows = pl.ds(pl.multiple_of(i * high, high), high)
            value = lax.dot_general(
                xp_ref[:, rows], mb_ref[...], (((0,), (0,)), ((), ())),
                preferred_element_type=F32,
            )
            for part in range(2 * pieces):
                n_ref[part, rows, :] = value[:, part * width:(part + 1) * width]

    near()
    for level in range(1, levels):
        for k in range(pieces):
            chain[level, k].wait_recv()
            tot_ref[level, k] = tot_ref[level - 1, k] + sums_ref[level - 1, k]
            if level + 1 < levels:
                chain[level + 1, k] = send(
                    tot_ref.at[level, k], sums_ref.at[level, k],
                    chain_send.at[level, k], chain_recv.at[level, k],
                    partner(level + 1), loop,
                )
            else:
                for way, there in enumerate(((loop + 1) % n_loop, (loop + n_loop - 1) % n_loop)):
                    chain["end", way, k] = send(
                        tot_ref.at[level, k], ends_ref.at[way, k],
                        end_send.at[way, k], end_recv.at[way, k], leaf, there,
                    )
        if level == 1:
            project()
            copy_n = send(
                n_ref.at[pl.ds(other, pieces)], nrecv_ref,
                early_send.at[pieces + 2], early_recv.at[pieces + 2], sibling, loop,
            )

    copy_c.wait_recv()
    copy_w.wait_recv()
    own = [doubled(c_ref[b]) for b in range(levels + 2)]
    theirs = [doubled(crecv_ref[b].astype(BF16)) for b in range(levels + 2)]
    both = [None] + [
        jnp.concatenate([own[b], theirs[b]], axis=0) for b in range(1, levels + 2)
    ]
    w_own, w_own_low = split(w_ref[...])
    w_sib, w_sib_low = split(wrecv_ref[...])
    w_high = jnp.concatenate([w_own, w_sib, w_own_low, w_sib_low], axis=1)
    partial_mix = []
    for k in range(pieces):
        value = jnp.concatenate([
            dot(own[0], stacked(sib_ref[k])),
            dot(theirs[0], stacked(coef_ref[mine + k])),
        ], axis=0)
        for level in range(1, levels):
            value = value + dot(both[level], stacked(sums_ref[level - 1, k]))
        partial_mix.append(value)
    copy_n.wait_recv()
    for k in range(pieces):
        f_ref[k] = (n_ref[mine + k] + nrecv_ref[k]).reshape(chips, chip_rows, width)

    bits = {}
    for k in range(pieces):
        order = list(range(chip_levels))
        bits[k] = order if k % 2 == 0 else order[::-1]

    def stage_tiles(k, stage):
        done = sum(2**bit for bit in bits[k][:stage])
        here = 2**bits[k][stage]
        found = [r for r in range(chips) if not r & done and r & here]
        later = bits[k][stage + 1:]
        found.sort(key=lambda r: [-((r >> bit) & 1) for bit in later])
        return found

    slots = {}
    for k in range(pieces):
        for stage in range(chip_levels):
            for r in stage_tiles(k, stage):
                slots[k, stage, r] = len([key for key in slots if key[0] == k])
    scatter = {}

    def launch(k, stage, r):
        bit = bits[k][stage]
        slot = slots[k, stage, r]
        scatter[k, stage, r] = send(
            f_ref.at[k, tile_of(r)], frecv_ref.at[k, slot],
            f_send.at[k, slot], f_recv.at[k, slot], partner(bit + 1), loop,
        )

    mix_copies = []
    for k in range(pieces):
        value = partial_mix[k]
        for way in range(2):
            chain["end", way, k].wait_recv()
            value = value + dot(both[levels + way], stacked(ends_ref[way, k]))
        rounded = value.astype(BF16)
        mixall_ref[mine + k] = rounded[:rank]
        mixsend_ref[k] = value[rank:]
        far = dot(w_high, jnp.concatenate([rounded, rounded], axis=0))
        f_ref[k] = f_ref[k] + far.reshape(chips, chip_rows, width)
        for r in stage_tiles(k, 0):
            launch(k, 0, r)
        mix_copies.append(send(
            mixsend_ref.at[k], mixrecv_ref.at[k], mix_send.at[k], mix_recv.at[k], sibling, loop
        ))

    for k in range(pieces):
        mix_copies[k].wait_recv()
        mixall_ref[other + k] = mixrecv_ref[k].astype(BF16)
    mix_all = jnp.concatenate([mixall_ref[part] for part in range(2 * pieces)], axis=1)

    @pl.loop(0, blocks)
    def finish(i):
        rows = pl.ds(pl.multiple_of(i * step, step), step)
        cross_ref[rows, :] = (m_ref[rows, :] + dot(u_ref[rows, :], mix_all)).astype(BF16)

    out_cross = pltpu.make_async_copy(cross_ref, cross_hbm.at[0], store_sem.at[0])
    out_cross.start()

    for stage in range(chip_levels):
        for k in range(pieces):
            here = 2**bits[k][stage]
            for r in stage_tiles(k, stage):
                scatter[k, stage, r].wait_recv()
                kept = r ^ here
                tile = tile_of(kept)
                f_ref[k, tile] = f_ref[k, tile] + frecv_ref[k, slots[k, stage, r]]
                if kept:
                    next_stage = stage + 1
                    if kept in stage_tiles(k, next_stage):
                        launch(k, next_stage, kept)

    z_copies = {}
    for k in range(pieces):
        value = f_ref[k, chip]
        for there in range(n_loop):
            zs_ref[k, there] = value[there * z_rows:(there + 1) * z_rows]
        for offset in range(1, n_loop):
            there = (loop + offset) % n_loop
            z_copies[k, offset] = send(
                zs_ref.at[k, there], zr_ref.at[offset - 1, k],
                z_send.at[offset - 1, k], z_recv.at[offset - 1, k], leaf, there,
            )
    for k in range(pieces):
        value = zs_ref[k, loop]
        for offset in range(1, n_loop):
            z_copies[k, offset].wait_recv()
            value = value + zr_ref[offset - 1, k]
        red_ref[k] = value

    place = loop % half_loop
    to_leaf = 2 * chip + owner

    def gather(offset):
        return pltpu.make_async_remote_copy(
            src_ref=red_ref, dst_ref=ag_ref.at[core, place],
            send_sem=ag_send.at[offset], recv_sem=ag_recv.at[core, place],
            device_id={"leaf": to_leaf, "loop": (loop + offset) % n_loop}, device_id_type=MESH,
        )

    for offset in range(1, n_loop):
        gather(offset).start()

    @pl.when(owner != core)
    def across():
        gather(0).start()

    for source in range(2):
        for at in range(half_loop):
            is_own = jnp.logical_and(source == core, core * half_loop + at == loop)

            @pl.when(is_own)
            def keep():
                for k in range(pieces):
                    ag_ref[source, at, k] = red_ref[k]

            @pl.when(jnp.logical_not(is_own))
            def arrive():
                pltpu.make_async_remote_copy(
                    src_ref=red_ref, dst_ref=ag_ref.at[source, at],
                    send_sem=ag_send.at[0], recv_sem=ag_recv.at[source, at],
                    device_id={"leaf": sibling, "loop": loop}, device_id_type=MESH,
                ).wait_recv()

            for k in range(pieces):
                left = (source * pieces + k) * width
                proj_ref[at * z_rows:(at + 1) * z_rows, left:left + width] = ag_ref[source, at, k]

    out_proj = pltpu.make_async_copy(proj_ref, proj_hbm, store_sem.at[1])
    out_proj.start()

    for copy in first + [copy_c, copy_w, copy_n] + mix_copies:
        copy.wait_send()
    for group in (chain, scatter, z_copies):
        for copy in group.values():
            copy.wait_send()
    for offset in range(1, n_loop):
        gather(offset).wait_send()

    @pl.when(owner != core)
    def drain():
        gather(0).wait_send()

    out_cross.wait()
    out_proj.wait()


def solution(mesh):
    n_leaf, n_loop = mesh.shape["leaf"], mesh.shape["loop"]
    levels = n_leaf.bit_length() - 1
    chips = n_leaf // 2

    def body(jacobian_t, leaf_block, left_basis, right_basis, couplings, group_coupling, obs_order):
        _, cells, obs = jacobian_t.shape
        rank = left_basis.shape[-1]
        width = 128
        pieces = obs // 2 // width
        chip_rows = obs // chips
        z_rows = chip_rows // n_loop
        half_loop = n_loop // 2
        anywhere = pl.BlockSpec(memory_space=pl.ANY)
        vmem = pltpu.VMEM
        dma = pltpu.SemaphoreType.DMA
        links = max(levels - 1, 1)
        return tuple(pl.pallas_call(
            functools.partial(kernel, n_leaf, n_loop),
            out_shape=(
                jax.ShapeDtypeStruct((1, cells, obs), BF16),
                jax.ShapeDtypeStruct((obs // n_leaf, obs), F32),
            ),
            in_specs=[anywhere] * 6 + [pl.BlockSpec(memory_space=pltpu.VMEM)],
            out_specs=(anywhere, anywhere),
            scratch_shapes=[
                vmem((cells, obs), BF16),
                vmem((cells, cells), BF16),
                vmem((cells, rank), BF16),
                vmem((cells, rank), BF16),
                vmem((levels + 2, rank, rank), BF16),
                vmem((cells, obs), BF16),
                vmem((cells, obs), F32),
                vmem((cells, obs), BF16),
                vmem((2 * pieces, obs, width), F32),
                vmem((pieces, obs, width), F32),
                vmem((2 * pieces, rank, width), F32),
                vmem((links, pieces, rank, width), F32),
                vmem((pieces, rank, width), F32),
                vmem((levels, pieces, rank, width), F32),
                vmem((2, pieces, rank, width), F32),
                vmem((levels + 2, rank, rank), F32),
                vmem((levels + 2, rank, rank), F32),
                vmem((obs, rank), F32),
                vmem((obs, rank), F32),
                vmem((pieces, rank, width), F32),
                vmem((pieces, rank, width), F32),
                vmem((2 * pieces, rank, width), BF16),
                vmem((pieces, chips, chip_rows, width), F32),
                vmem((pieces, chips, chip_rows, width), F32),
                vmem((pieces, n_loop, z_rows, width), F32),
                vmem((n_loop - 1, pieces, z_rows, width), F32),
                vmem((pieces, z_rows, width), F32),
                vmem((2, half_loop, pieces, z_rows, width), F32),
                vmem((cells, obs), BF16),
                vmem((obs // n_leaf, obs), F32),
                dma((6,)),
                dma((2,)),
                dma((pieces + 3,)),
                dma((pieces + 3,)),
                dma((links, pieces)),
                dma((links, pieces)),
                dma((2, pieces)),
                dma((2, pieces)),
                dma((pieces,)),
                dma((pieces,)),
                dma((pieces, chips)),
                dma((pieces, chips)),
                dma((n_loop - 1, pieces)),
                dma((n_loop - 1, pieces)),
                dma((n_loop,)),
                dma((2, half_loop)),
            ],
            compiler_params=pltpu.CompilerParams(
                collective_id=0, has_side_effects=True, vmem_limit_bytes=60 * 2**20,
            ),
        )(jacobian_t, leaf_block, left_basis, right_basis, couplings, group_coupling,
          obs_order.reshape(1, obs)))

    in_specs = (
        P("loop", "leaf", None),
        P("loop", "leaf", None),
        P("loop", "leaf", None),
        P("loop", "leaf", None),
        P("loop", "leaf", None, None),
        P("loop", "leaf", None, None),
        P(),
    )
    out_specs = (P("loop", "leaf", None), P("leaf", None))
    return jax.shard_map(body, mesh=mesh, in_specs=in_specs, out_specs=out_specs, check_vma=False)
```

time: 132 us -> 42 us (0.32)
  the two profiles are of different devices: /device:TPU:0 before, /device:TPU:1 now
where the time goes in v1:
time: 42 us; the launch traced here: 41.7 us
  Pallas kernels  38.1 us (91%)
  local copies, waits for them, and re-layouts  2.96 us (7%)
  between operations  0.65 us (2%)
    pallas_call x1, Pallas kernels, body(): pl.pallas_call(functools.partial(kernel, n_leaf, n_loop), out_shape=(jax....  38.1 us
    unnamed x4, local copies, waits for them, and re-layouts  2.96 us

profile of v1, /device:TPU:1, one launch (start us, length us, event | category | flops | bytes accessed | tf_op | source)
XLA Modules:
  0.0 41.7 jit_solution(15962625699514637494)
XLA Ops:
  0.6 38.1 %shard_map.86 = (bf16[1,1024,512]{2,1,0:T(8,128)(2,1)}, f32[64,512]{1,0:T(8,128)}) custom-call(bf16[1,1024,512]{2,1,0:T(8,128)(2,1)} %x_hbm.1, bf16[1,1024,1024]{2,1,0:T(8,128)(2,1)} %l_hbm.1, bf16[1,1024,128]{2,1,0:T(8,128)(2,1)} %u_hbm.1, bf16[1,1024,128]{2,1,0:T(8,128)(2,1)} %v_hbm.1, bf16[1,3,128,128]{3,2,1,0:T(8,128)(2,1)} %c_hbm.1, ...), custom_call_target="tpu_custom_call" | custom-call | tf_op jit(solution)/shard_map/pallas_call | solution.py:384
  38.8 0.0 copy-start
  38.8 2.3 %copy.11 = bf16[1,1024,512]{2,1,0:T(8,128)(2,1)} copy(bf16[1,1024,512]{2,1,0:T(8,128)(2,1)} %get-tuple-element.4) | data formatting | bytes 2097152
  41.1 0.0 copy-done
  41.1 0.7 %copy.12 = f32[64,512]{1,0:T(8,128)} copy(f32[64,512]{1,0:T(8,128)S(1)} %copy-done) | data formatting | bytes 262144
Async XLA Ops:
  38.8 2.3 %copy-start = (f32[64,512]{1,0:T(8,128)S(1)}, f32[64,512]{1,0:T(8,128)}, u32[]{:S(2)}) copy-start(f32[64,512]{1,0:T(8,128)} %get-tuple-element.5) | copy-start | bytes 393220

commit v2 on v1

v2 whole, which is shorter than its diff:
```python
import functools

import jax
import jax.numpy as jnp
from jax import lax
from jax.experimental import pallas as pl
from jax.experimental.pallas import tpu as pltpu
from jax.sharding import PartitionSpec as P

MESH = pl.DeviceIdType.MESH
F32 = jnp.float32
BF16 = jnp.bfloat16


def dot(a, b):
    return jnp.dot(a, b, preferred_element_type=F32)


def split(value):
    high = value.astype(BF16)
    low = (value - high.astype(F32)).astype(BF16)
    return high, low


def stacked(value):
    return jnp.concatenate(split(value), axis=0)


def doubled(value):
    return jnp.concatenate([value, value], axis=1)


def kernel(
    n_leaf, n_loop, halves, x_hbm, l_hbm, u_hbm, v_hbm, c_hbm, g_hbm, order_ref,
    cross_hbm, proj_hbm,
    x_ref, l_ref, u_ref, v_ref, c_ref, xp_ref, m_ref, mb_ref, n_ref, nrecv_ref,
    coef_ref, sums_ref, sib_ref, tot_ref, ends_ref, csend_ref, crecv_ref,
    w_ref, wrecv_ref, mixsend_ref, mixrecv_ref, mixall_ref,
    f_ref, frecv_ref, zs_ref, zr_ref, red_ref, ag_ref, cross_ref, proj_ref,
    load_sem, store_sem, early_send, early_recv, chain_send, chain_recv,
    end_send, end_recv, mix_send, mix_recv, f_send, f_recv, z_send, z_recv,
    ag_send, ag_recv, wcat_ref, part_ref, qs_ref, qz_ref, qt_ref, q_send, q_recv,
):
    levels = n_leaf.bit_length() - 1
    chips = n_leaf // 2
    chip_levels = levels - 1
    pieces, rank, width = sums_ref.shape[1:]
    cells, obs = x_ref.shape
    chip_rows = obs // chips
    z_rows = chip_rows // n_loop
    half_loop = n_loop // 2
    leaf = lax.axis_index("leaf")
    loop = lax.axis_index("loop")
    core = leaf % 2
    chip = leaf // 2
    sibling = leaf + 1 - 2 * core
    owner = loop // half_loop

    def partner(bit):
        mask = 2**bit
        return leaf + mask * (1 - 2 * ((leaf // mask) % 2))

    def tile_of(relative):
        index = 0
        for bit in range(chip_levels):
            step = 2**bit
            index = index + step * (((chip // step) + (relative // step) % 2) % 2)
        return index

    def send(src, dst, send_sem, recv_sem, to_leaf, to_loop):
        copy = pltpu.make_async_remote_copy(
            src_ref=src, dst_ref=dst, send_sem=send_sem, recv_sem=recv_sem,
            device_id={"leaf": to_leaf, "loop": to_loop}, device_id_type=MESH,
        )
        copy.start()
        return copy

    loads = []
    for number, (src, dst) in enumerate((
        (v_hbm.at[0], v_ref), (x_hbm.at[0], x_ref),
        (u_hbm.at[0], u_ref), (c_hbm.at[0], c_ref.at[pl.ds(0, levels)]),
        (g_hbm.at[0], c_ref.at[pl.ds(levels, 2)]), (l_hbm.at[0], l_ref),
    )):
        loads.append(pltpu.make_async_copy(src, dst, load_sem.at[number]))
        loads[-1].start()

    barrier = pltpu.get_barrier_semaphore()
    for bit in range(1, levels):
        pl.semaphore_signal(
            barrier, inc=1, device_id={"leaf": partner(bit), "loop": loop}, device_id_type=MESH
        )
    for offset in range(n_loop):
        there = (loop + offset) % n_loop
        for to_leaf in (leaf, sibling):
            if offset or to_leaf is sibling:
                pl.semaphore_signal(
                    barrier, inc=1, device_id={"leaf": to_leaf, "loop": there}, device_id_type=MESH
                )

    loads[0].wait()
    loads[1].wait()
    coef = lax.dot_general(
        v_ref[...], x_ref[...], (((0,), (0,)), ((), ())), preferred_element_type=F32
    )
    for part in range(2 * pieces):
        coef_ref[part] = coef[:, part * width:(part + 1) * width]
    pl.semaphore_wait(barrier, levels - 1 + 2 * n_loop - 1)
    mine, other = core * pieces, (1 - core) * pieces
    sent = []
    first = []
    for k in range(pieces):
        first.append(send(
            coef_ref.at[other + k], sib_ref.at[k], early_send.at[k], early_recv.at[k],
            sibling, loop,
        ))

    loads[3].wait()
    loads[4].wait()
    csend_ref[...] = c_ref[...].astype(F32)
    copy_c = send(
        csend_ref, crecv_ref, early_send.at[pieces], early_recv.at[pieces], sibling, loop
    )
    chain = {}
    high = rank // halves

    def rows_of(half):
        return pl.ds(half * high, high)

    def advance(level, k, half):
        rows = rows_of(half)
        if level + 1 < levels:
            chain[level + 1, k, half] = send(
                tot_ref.at[level, k, rows], sums_ref.at[level, k, rows],
                chain_send.at[level, k, half], chain_recv.at[level, k, half],
                partner(level + 1), loop,
            )
            return
        for way, there in enumerate(((loop + 1) % n_loop, (loop + n_loop - 1) % n_loop)):
            chain["end", way, k, half] = send(
                tot_ref.at[level, k, rows], ends_ref.at[way, k, rows],
                end_send.at[way, k, half], end_recv.at[way, k, half], leaf, there,
            )

    for k in range(pieces):
        first[k].wait_recv()
        tot_ref[0, k] = coef_ref[mine + k] + sib_ref[k]
        for half in range(halves):
            advance(0, k, half)

    onehot = (
        lax.broadcasted_iota(jnp.int32, (obs, obs), 0)
        == jnp.broadcast_to(order_ref[...], (obs, obs))
    ).astype(F32).astype(BF16)
    blocks = 4
    step = cells // blocks

    @pl.loop(0, blocks)
    def permute(i):
        rows = pl.ds(pl.multiple_of(i * step, step), step)
        xp_ref[rows, :] = dot(x_ref[rows, :], onehot).astype(BF16)

    loads[2].wait()
    w_ref[...] = lax.dot_general(
        xp_ref[...], u_ref[...], (((0,), (0,)), ((), ())), preferred_element_type=F32
    )
    copy_w = send(
        w_ref, wrecv_ref, early_send.at[pieces + 1], early_recv.at[pieces + 1], sibling, loop
    )

    bits = {}
    for k in range(pieces + 1):
        order = list(range(chip_levels))
        bits[k] = order if k % 2 == 0 else order[::-1]

    def stage_tiles(k, stage):
        done = sum(2**bit for bit in bits[k][:stage])
        here = 2**bits[k][stage]
        found = [r for r in range(chips) if not r & done and r & here]
        later = bits[k][stage + 1:]
        found.sort(key=lambda r: [-((r >> bit) & 1) for bit in later])
        return found

    slots = {}
    for k in range(pieces + 1):
        for stage in range(chip_levels):
            for r in stage_tiles(k, stage):
                slots[k, stage, r] = len([key for key in slots if key[0] == k])
    scatter = {}

    def launch(k, stage, r):
        bit = bits[k][stage]
        slot = slots[k, stage, r]
        scatter[k, stage, r] = send(
            f_ref.at[k, tile_of(r)], frecv_ref.at[k, slot],
            f_send.at[k, slot], f_recv.at[k, slot], partner(bit + 1), loop,
        )

    def collect(k, stage):
        here = 2**bits[k][stage]
        for r in stage_tiles(k, stage):
            scatter[k, stage, r].wait_recv()
            kept = r ^ here
            tile = tile_of(kept)
            f_ref[k, tile] = f_ref[k, tile] + frecv_ref[k, slots[k, stage, r]]
            if kept and kept in stage_tiles(k, stage + 1):
                launch(k, stage + 1, kept)

    def near():
        @pl.loop(0, blocks)
        def multiply(i):
            rows = pl.ds(pl.multiple_of(i * step, step), step)
            value = dot(l_ref[rows, :], x_ref[...])
            m_ref[rows, :] = value
            mb_ref[rows, :] = value.astype(BF16)

    def project():
        tall = obs // blocks

        @pl.loop(0, blocks)
        def multiply(i):
            rows = pl.ds(pl.multiple_of(i * tall, tall), tall)
            value = lax.dot_general(
                xp_ref[:, rows], mb_ref[...], (((0,), (0,)), ((), ())),
                preferred_element_type=F32,
            )
            for part in range(2 * pieces):
                n_ref[part, rows, :] = value[:, part * width:(part + 1) * width]

    extra = pieces
    for level in range(1, levels):
        for k in range(pieces):
            for half in range(halves):
                rows = rows_of(half)
                chain[level, k, half].wait_recv()
                tot_ref[level, k, rows] = tot_ref[level - 1, k, rows] + sums_ref[level - 1, k, rows]
                advance(level, k, half)
        if level == 1:
            copy_c.wait_recv()
            copy_w.wait_recv()
            w_own, w_own_low = split(w_ref[...])
            w_sib, w_sib_low = split(wrecv_ref[...])
            w_high = jnp.concatenate([w_own, w_sib, w_own_low, w_sib_low], axis=1)
            wcat_ref[...] = w_high
            g_own, g_sib = c_ref[levels + core], crecv_ref[levels + core].astype(BF16)
            reach = dot(w_high, jnp.concatenate([g_own, g_sib, g_own, g_sib], axis=0))
            f_ref[extra] = reach.reshape(chips, chip_rows, width)
            for r in stage_tiles(extra, 0):
                launch(extra, 0, r)
            loads[5].wait()
            near()
            project()
            copy_n = send(
                n_ref.at[pl.ds(other, pieces)], nrecv_ref,
                early_send.at[pieces + 2], early_recv.at[pieces + 2], sibling, loop,
            )

    own = [doubled(c_ref[b]) for b in range(levels)]
    theirs = [doubled(crecv_ref[b].astype(BF16)) for b in range(levels)]
    for k in range(pieces):
        value = jnp.concatenate([
            dot(own[0], stacked(sib_ref[k])),
            dot(theirs[0], stacked(coef_ref[mine + k])),
        ], axis=0)
        for level in range(1, levels):
            both = jnp.concatenate([own[level], theirs[level]], axis=0)
            value = value + dot(both, stacked(sums_ref[level - 1, k]))
        part_ref[k] = value
        rounded = value.astype(BF16)
        far = dot(wcat_ref[...], jnp.concatenate([rounded, rounded], axis=0))
        if k == 0:
            copy_n.wait_recv()
        f_ref[k] = (n_ref[mine + k] + nrecv_ref[k] + far).reshape(chips, chip_rows, width)
        for r in stage_tiles(k, 0):
            launch(k, 0, r)

    for stage in range(chip_levels):
        collect(extra, stage)
    qs_ref[...] = f_ref[extra, chip]
    copy_q = send(
        qs_ref, qz_ref, q_send.at[0], q_recv.at[0],
        leaf, (loop + n_loop - 1 + 2 * core) % n_loop,
    )
    for stage in range(chip_levels - 1):
        for k in range(pieces):
            collect(k, stage)
    copy_q.wait_recv()
    copy_t = send(qz_ref, qt_ref, q_send.at[1], q_recv.at[1], sibling, loop)
    copy_t.wait_recv()
    a_high, a_low = split(qz_ref[...] + qt_ref[...])
    a_all = jnp.concatenate([a_high, a_low, a_high], axis=1)

    z_copies = {}
    for k in range(pieces):
        t_high, t_low = split(tot_ref[levels - 1, k])
        reached = dot(a_all, jnp.concatenate([t_high, t_high, t_low], axis=0))
        if chip_levels:
            collect(k, chip_levels - 1)
        value = f_ref[k, chip] + reached
        for there in range(n_loop):
            zs_ref[k, there] = value[there * z_rows:(there + 1) * z_rows]
        for offset in range(1, n_loop):
            there = (loop + offset) % n_loop
            z_copies[k, offset] = send(
                zs_ref.at[k, there], zr_ref.at[offset - 1, k],
                z_send.at[offset - 1, k], z_recv.at[offset - 1, k], leaf, there,
            )

    mix_copies = []
    for k in range(pieces):
        value = part_ref[k]
        for way in range(2):
            for half in range(halves):
                chain["end", way, k, half].wait_recv()
            both = jnp.concatenate([
                doubled(c_ref[levels + way]), doubled(crecv_ref[levels + way].astype(BF16)),
            ], axis=0)
            value = value + dot(both, stacked(ends_ref[way, k]))
        mixall_ref[mine + k] = value[:rank].astype(BF16)
        mixsend_ref[k] = value[rank:]
        mix_copies.append(send(
            mixsend_ref.at[k], mixrecv_ref.at[k], mix_send.at[k], mix_recv.at[k], sibling, loop
        ))

    place = loop % half_loop
    to_leaf = 2 * chip + owner

    def gather(offset, k):
        return pltpu.make_async_remote_copy(
            src_ref=red_ref.at[k], dst_ref=ag_ref.at[core, place, k],
            send_sem=ag_send.at[offset, k], recv_sem=ag_recv.at[core, place, k],
            device_id={"leaf": to_leaf, "loop": (loop + offset) % n_loop}, device_id_type=MESH,
        )

    for k in range(pieces):
        value = zs_ref[k, loop]
        for offset in range(1, n_loop):
            z_copies[k, offset].wait_recv()
            value = value + zr_ref[offset - 1, k]
        red_ref[k] = value
        for offset in range(1, n_loop):
            gather(offset, k).start()

        @pl.when(owner != core)
        def across():
            gather(0, k).start()

    for k in range(pieces):
        mix_copies[k].wait_recv()
        mixall_ref[other + k] = mixrecv_ref[k].astype(BF16)
    mix_all = jnp.concatenate([mixall_ref[part] for part in range(2 * pieces)], axis=1)

    @pl.loop(0, blocks)
    def finish(i):
        rows = pl.ds(pl.multiple_of(i * step, step), step)
        cross_ref[rows, :] = (m_ref[rows, :] + dot(u_ref[rows, :], mix_all)).astype(BF16)

    out_cross = pltpu.make_async_copy(cross_ref, cross_hbm.at[0], store_sem.at[0])
    out_cross.start()

    for k in range(pieces):
        for source in range(2):
            for at in range(half_loop):
                is_own = jnp.logical_and(source == core, core * half_loop + at == loop)

                @pl.when(is_own)
                def keep():
                    ag_ref[source, at, k] = red_ref[k]

                @pl.when(jnp.logical_not(is_own))
                def arrive():
                    pltpu.make_async_remote_copy(
                        src_ref=red_ref.at[k], dst_ref=ag_ref.at[source, at, k],
                        send_sem=ag_send.at[0, k], recv_sem=ag_recv.at[source, at, k],
                        device_id={"leaf": sibling, "loop": loop}, device_id_type=MESH,
                    ).wait_recv()

                left = (source * pieces + k) * width
                proj_ref[at * z_rows:(at + 1) * z_rows, left:left + width] = ag_ref[source, at, k]

    out_proj = pltpu.make_async_copy(proj_ref, proj_hbm, store_sem.at[1])
    out_proj.start()

    for copy in first + [copy_c, copy_w, copy_n, copy_q, copy_t] + mix_copies:
        copy.wait_send()
    for group in (chain, scatter, z_copies):
        for copy in group.values():
            copy.wait_send()
    for k in range(pieces):
        for offset in range(1, n_loop):
            gather(offset, k).wait_send()

        @pl.when(owner != core)
        def drain():
            gather(0, k).wait_send()

    out_cross.wait()
    out_proj.wait()


def solution(mesh):
    n_leaf, n_loop = mesh.shape["leaf"], mesh.shape["loop"]
    levels = n_leaf.bit_length() - 1
    chips = n_leaf // 2

    def body(jacobian_t, leaf_block, left_basis, right_basis, couplings, group_coupling, obs_order):
        _, cells, obs = jacobian_t.shape
        rank = left_basis.shape[-1]
        width = 128
        pieces = obs // 2 // width
        chip_rows = obs // chips
        z_rows = chip_rows // n_loop
        half_loop = n_loop // 2
        halves = 2
        anywhere = pl.BlockSpec(memory_space=pl.ANY)
        vmem = pltpu.VMEM
        dma = pltpu.SemaphoreType.DMA
        links = max(levels - 1, 1)
        return tuple(pl.pallas_call(
            functools.partial(kernel, n_leaf, n_loop, halves),
            out_shape=(
                jax.ShapeDtypeStruct((1, cells, obs), BF16),
                jax.ShapeDtypeStruct((obs // n_leaf, obs), F32),
            ),
            in_specs=[anywhere] * 6 + [pl.BlockSpec(memory_space=pltpu.VMEM)],
            out_specs=(anywhere, anywhere),
            scratch_shapes=[
                vmem((cells, obs), BF16),
                vmem((cells, cells), BF16),
                vmem((cells, rank), BF16),
                vmem((cells, rank), BF16),
                vmem((levels + 2, rank, rank), BF16),
                vmem((cells, obs), BF16),
                vmem((cells, obs), F32),
                vmem((cells, obs), BF16),
                vmem((2 * pieces, obs, width), F32),
                vmem((pieces, obs, width), F32),
                vmem((2 * pieces, rank, width), F32),
                vmem((links, pieces, rank, width), F32),
                vmem((pieces, rank, width), F32),
                vmem((levels, pieces, rank, width), F32),
                vmem((2, pieces, rank, width), F32),
                vmem((levels + 2, rank, rank), F32),
                vmem((levels + 2, rank, rank), F32),
                vmem((obs, rank), F32),
                vmem((obs, rank), F32),
                vmem((pieces, rank, width), F32),
                vmem((pieces, rank, width), F32),
                vmem((2 * pieces, rank, width), BF16),
                vmem((pieces + 1, chips, chip_rows, width), F32),
                vmem((pieces + 1, chips, chip_rows, width), F32),
                vmem((pieces, n_loop, z_rows, width), F32),
                vmem((n_loop - 1, pieces, z_rows, width), F32),
                vmem((pieces, z_rows, width), F32),
                vmem((2, half_loop, pieces, z_rows, width), F32),
                vmem((cells, obs), BF16),
                vmem((obs // n_leaf, obs), F32),
                dma((6,)),
                dma((2,)),
                dma((pieces + 3,)),
                dma((pieces + 3,)),
                dma((links, pieces, halves)),
                dma((links, pieces, halves)),
                dma((2, pieces, halves)),
                dma((2, pieces, halves)),
                dma((pieces,)),
                dma((pieces,)),
                dma((pieces + 1, chips)),
                dma((pieces + 1, chips)),
                dma((n_loop - 1, pieces)),
                dma((n_loop - 1, pieces)),
                dma((n_loop, pieces)),
                dma((2, half_loop, pieces)),
                vmem((obs, 4 * rank), BF16),
                vmem((pieces, 2 * rank, width), F32),
                vmem((chip_rows, width), F32),
                vmem((chip_rows, width), F32),
                vmem((chip_rows, width), F32),
                dma((2,)),
                dma((2,)),
            ],
            compiler_params=pltpu.CompilerParams(
                collective_id=0, has_side_effects=True, vmem_limit_bytes=60 * 2**20,
            ),
        )(jacobian_t, leaf_block, left_basis, right_basis, couplings, group_coupling,
          obs_order.reshape(1, obs)))

    in_specs = (
        P("loop", "leaf", None),
        P("loop", "leaf", None),
        P("loop", "leaf", None),
        P("loop", "leaf", None),
        P("loop", "leaf", None, None),
        P("loop", "leaf", None, None),
        P(),
    )
    out_specs = (P("loop", "leaf", None), P("leaf", None))
    return jax.shard_map(body, mesh=mesh, in_specs=in_specs, out_specs=out_specs, check_vma=False)
```

time: 42 us -> 42.8 us (1.019)
  Pallas kernels: 38.1 us -> 39 us
    pallas_call x1, Pallas kernels: 38.1 us -> 39 us  [body(): pl.pallas_call(functools.partial(kernel, n_leaf, n_loop, halves), out_sha...]
where the time goes in v2:
time: 42.8 us; the launch traced here: 42.6 us
  Pallas kernels  39 us (91%)
  local copies, waits for them, and re-layouts  2.96 us (7%)
  between operations  0.65 us (2%)
    pallas_call x1, Pallas kernels, body(): pl.pallas_call(functools.partial(kernel, n_leaf, n_loop, halves), out_sha...  39 us
    unnamed x4, local copies, waits for them, and re-layouts  2.96 us

profile of v2, /device:TPU:1, one launch (start us, length us, event | category | flops | bytes accessed | tf_op | source)
XLA Modules:
  0.0 42.6 jit_solution(12122238494080412325)
XLA Ops:
  0.6 39.0 %shard_map.86 = (bf16[1,1024,512]{2,1,0:T(8,128)(2,1)}, f32[64,512]{1,0:T(8,128)}) custom-call(bf16[1,1024,512]{2,1,0:T(8,128)(2,1)} %x_hbm.1, bf16[1,1024,1024]{2,1,0:T(8,128)(2,1)} %l_hbm.1, bf16[1,1024,128]{2,1,0:T(8,128)(2,1)} %u_hbm.1, bf16[1,1024,128]{2,1,0:T(8,128)(2,1)} %v_hbm.1, bf16[1,3,128,128]{3,2,1,0:T(8,128)(2,1)} %c_hbm.1, ...), custom_call_target="tpu_custom_call" | custom-call | tf_op jit(solution)/shard_map/pallas_call | solution.py:418
  39.6 0.0 copy-start
  39.6 2.3 %copy.11 = bf16[1,1024,512]{2,1,0:T(8,128)(2,1)} copy(bf16[1,1024,512]{2,1,0:T(8,128)(2,1)} %get-tuple-element.4) | data formatting | bytes 2097152
  41.9 0.0 copy-done
  42.0 0.7 %copy.12 = f32[64,512]{1,0:T(8,128)} copy(f32[64,512]{1,0:T(8,128)S(1)} %copy-done) | data formatting | bytes 262144
Async XLA Ops:
  39.6 2.3 %copy-start = (f32[64,512]{1,0:T(8,128)S(1)}, f32[64,512]{1,0:T(8,128)}, u32[]{:S(2)}) copy-start(f32[64,512]{1,0:T(8,128)} %get-tuple-element.5) | copy-start | bytes 393220

commit v3 on v2

--- a/solution.py
+++ b/solution.py
@@ -39,7 +39,7 @@
     f_ref, frecv_ref, zs_ref, zr_ref, red_ref, ag_ref, cross_ref, proj_ref,
     load_sem, store_sem, early_send, early_recv, chain_send, chain_recv,
     end_send, end_recv, mix_send, mix_recv, f_send, f_recv, z_send, z_recv,
-    ag_send, ag_recv, wcat_ref, part_ref, qs_ref, qz_ref, qt_ref, q_send, q_recv,
+    ag_send, ag_recv, wcat_ref, part_ref, qs_ref, qz_ref, q_send, q_recv,
 ):
     levels = n_leaf.bit_length() - 1
     chips = n_leaf // 2
@@ -141,12 +141,6 @@
                 end_send.at[way, k, half], end_recv.at[way, k, half], leaf, there,
             )
 
-    for k in range(pieces):
-        first[k].wait_recv()
-        tot_ref[0, k] = coef_ref[mine + k] + sib_ref[k]
-        for half in range(halves):
-            advance(0, k, half)
-
     onehot = (
         lax.broadcasted_iota(jnp.int32, (obs, obs), 0)
         == jnp.broadcast_to(order_ref[...], (obs, obs))
@@ -158,6 +152,12 @@
     def permute(i):
         rows = pl.ds(pl.multiple_of(i * step, step), step)
         xp_ref[rows, :] = dot(x_ref[rows, :], onehot).astype(BF16)
+
+    for k in range(pieces):
+        first[k].wait_recv()
+        tot_ref[0, k] = coef_ref[mine + k] + sib_ref[k]
+        for half in range(halves):
+            advance(0, k, half)
 
     loads[2].wait()
     w_ref[...] = lax.dot_general(
@@ -205,26 +205,43 @@
             if kept and kept in stage_tiles(k, stage + 1):
                 launch(k, stage + 1, kept)
 
-    def near():
-        @pl.loop(0, blocks)
-        def multiply(i):
-            rows = pl.ds(pl.multiple_of(i * step, step), step)
-            value = dot(l_ref[rows, :], x_ref[...])
-            m_ref[rows, :] = value
-            mb_ref[rows, :] = value.astype(BF16)
-
-    def project():
-        tall = obs // blocks
-
-        @pl.loop(0, blocks)
-        def multiply(i):
-            rows = pl.ds(pl.multiple_of(i * tall, tall), tall)
-            value = lax.dot_general(
-                xp_ref[:, rows], mb_ref[...], (((0,), (0,)), ((), ())),
-                preferred_element_type=F32,
-            )
-            for part in range(2 * pieces):
-                n_ref[part, rows, :] = value[:, part * width:(part + 1) * width]
+    loads[5].wait()
+    tall = obs // blocks
+
+    def near(i):
+        rows = pl.ds(i * step, step)
+        value = dot(l_ref[rows, :], x_ref[...])
+        m_ref[rows, :] = value
+        mb_ref[rows, :] = value.astype(BF16)
+
+    def project(i):
+        rows = pl.ds(i * tall, tall)
+        value = lax.dot_general(
+            xp_ref[:, rows], mb_ref[...], (((0,), (0,)), ((), ())), preferred_element_type=F32
+        )
+        for part in range(2 * pieces):
+            n_ref[part, rows, :] = value[:, part * width:(part + 1) * width]
+
+    jobs = [functools.partial(near, i) for i in range(blocks)]
+    jobs += [functools.partial(project, i) for i in range(blocks)]
+
+    def work(count):
+        for job in jobs[:count]:
+            job()
+        del jobs[:count]
+
+    work(2)
+    copy_c.wait_recv()
+    copy_w.wait_recv()
+    w_own, w_own_low = split(w_ref[...])
+    w_sib, w_sib_low = split(wrecv_ref[...])
+    w_high = jnp.concatenate([w_own, w_sib, w_own_low, w_sib_low], axis=1)
+    wcat_ref[...] = w_high
+    g_own, g_sib = c_ref[levels + core], crecv_ref[levels + core].astype(BF16)
+    reach = dot(w_high, jnp.concatenate([g_own, g_sib, g_own, g_sib], axis=0))
+    f_ref[pieces] = reach.reshape(chips, chip_rows, width)
+    for r in stage_tiles(pieces, 0):
+        launch(pieces, 0, r)
 
     extra = pieces
     for level in range(1, levels):
@@ -233,27 +250,18 @@
                 rows = rows_of(half)
                 chain[level, k, half].wait_recv()
                 tot_ref[level, k, rows] = tot_ref[level - 1, k, rows] + sums_ref[level - 1, k, rows]
-                advance(level, k, half)
+                if level + 1 < levels:
+                    advance(level, k, half)
+                work(1)
+        work(len(jobs))
         if level == 1:
-            copy_c.wait_recv()
-            copy_w.wait_recv()
-            w_own, w_own_low = split(w_ref[...])
-            w_sib, w_sib_low = split(wrecv_ref[...])
-            w_high = jnp.concatenate([w_own, w_sib, w_own_low, w_sib_low], axis=1)
-            wcat_ref[...] = w_high
-            g_own, g_sib = c_ref[levels + core], crecv_ref[levels + core].astype(BF16)
-            reach = dot(w_high, jnp.concatenate([g_own, g_sib, g_own, g_sib], axis=0))
-            f_ref[extra] = reach.reshape(chips, chip_rows, width)
-            for r in stage_tiles(extra, 0):
-                launch(extra, 0, r)
-            loads[5].wait()
-            near()
-            project()
             copy_n = send(
                 n_ref.at[pl.ds(other, pieces)], nrecv_ref,
                 early_send.at[pieces + 2], early_recv.at[pieces + 2], sibling, loop,
             )
 
+    if chip_levels > 1:
+        collect(extra, 0)
     own = [doubled(c_ref[b]) for b in range(levels)]
     theirs = [doubled(crecv_ref[b].astype(BF16)) for b in range(levels)]
     for k in range(pieces):
@@ -273,20 +281,26 @@
         for r in stage_tiles(k, 0):
             launch(k, 0, r)
 
-    for stage in range(chip_levels):
+    for stage in range(1 if chip_levels > 1 else 0, chip_levels):
         collect(extra, stage)
     qs_ref[...] = f_ref[extra, chip]
-    copy_q = send(
-        qs_ref, qz_ref, q_send.at[0], q_recv.at[0],
-        leaf, (loop + n_loop - 1 + 2 * core) % n_loop,
-    )
+    q_there = (loop + n_loop - 1 + 2 * core) % n_loop
+    copy_q = [
+        send(qs_ref, qz_ref.at[core], q_send.at[at], q_recv.at[core], to_leaf, q_there)
+        for at, to_leaf in enumerate((leaf, sibling))
+    ]
+    for k in range(pieces):
+        for half in range(halves):
+            advance(levels - 1, k, half)
     for stage in range(chip_levels - 1):
         for k in range(pieces):
             collect(k, stage)
-    copy_q.wait_recv()
-    copy_t = send(qz_ref, qt_ref, q_send.at[1], q_recv.at[1], sibling, loop)
-    copy_t.wait_recv()
-    a_high, a_low = split(qz_ref[...] + qt_ref[...])
+    for at in range(2):
+        pltpu.make_async_remote_copy(
+            src_ref=qs_ref, dst_ref=qz_ref.at[at], send_sem=q_send.at[at], recv_sem=q_recv.at[at],
+            device_id={"leaf": sibling, "loop": loop}, device_id_type=MESH,
+        ).wait_recv()
+    a_high, a_low = split(qz_ref[0] + qz_ref[1])
     a_all = jnp.concatenate([a_high, a_low, a_high], axis=1)
 
     z_copies = {}
@@ -380,7 +394,7 @@
     out_proj = pltpu.make_async_copy(proj_ref, proj_hbm, store_sem.at[1])
     out_proj.start()
 
-    for copy in first + [copy_c, copy_w, copy_n, copy_q, copy_t] + mix_copies:
+    for copy in first + [copy_c, copy_w, copy_n] + copy_q + mix_copies:
         copy.wait_send()
     for group in (chain, scatter, z_copies):
         for copy in group.values():
@@ -473,8 +487,7 @@
                 vmem((obs, 4 * rank), BF16),
                 vmem((pieces, 2 * rank, width), F32),
                 vmem((chip_rows, width), F32),
-                vmem((chip_rows, width), F32),
-                vmem((chip_rows, width), F32),
+                vmem((2, chip_rows, width), F32),
                 dma((2,)),
                 dma((2,)),
             ],

time: 42.8 us -> 38.5 us (0.90)
  Pallas kernels: 39 us -> 34.7 us
    pallas_call x1, Pallas kernels: 39 us -> 34.7 us  [body(): pl.pallas_call(functools.partial(kernel, n_leaf, n_loop, halves), out_sha...]
where the time goes in v3:
time: 38.5 us; the launch traced here: 38.3 us
  Pallas kernels  34.7 us (90%)
  local copies, waits for them, and re-layouts  2.96 us (8%)
  between operations  0.65 us (2%)
    pallas_call x1, Pallas kernels, body(): pl.pallas_call(functools.partial(kernel, n_leaf, n_loop, halves), out_sha...  34.7 us
    unnamed x4, local copies, waits for them, and re-layouts  2.96 us

profile of v3, /device:TPU:1, one launch (start us, length us, event | category | flops | bytes accessed | tf_op | source)
XLA Modules:
  0.0 38.3 jit_solution(14659677417658866545)
XLA Ops:
  0.6 34.7 %shard_map.86 = (bf16[1,1024,512]{2,1,0:T(8,128)(2,1)}, f32[64,512]{1,0:T(8,128)}) custom-call(bf16[1,1024,512]{2,1,0:T(8,128)(2,1)} %x_hbm.1, bf16[1,1024,1024]{2,1,0:T(8,128)(2,1)} %l_hbm.1, bf16[1,1024,128]{2,1,0:T(8,128)(2,1)} %u_hbm.1, bf16[1,1024,128]{2,1,0:T(8,128)(2,1)} %v_hbm.1, bf16[1,3,128,128]{3,2,1,0:T(8,128)(2,1)} %c_hbm.1, ...), custom_call_target="tpu_custom_call" | custom-call | tf_op jit(solution)/shard_map/pallas_call | solution.py:432
  35.3 0.0 copy-start
  35.3 2.3 %copy.11 = bf16[1,1024,512]{2,1,0:T(8,128)(2,1)} copy(bf16[1,1024,512]{2,1,0:T(8,128)(2,1)} %get-tuple-element.4) | data formatting | bytes 2097152
  37.6 0.0 copy-done
  37.6 0.7 %copy.12 = f32[64,512]{1,0:T(8,128)} copy(f32[64,512]{1,0:T(8,128)S(1)} %copy-done) | data formatting | bytes 262144
Async XLA Ops:
  35.3 2.3 %copy-start = (f32[64,512]{1,0:T(8,128)S(1)}, f32[64,512]{1,0:T(8,128)}, u32[]{:S(2)}) copy-start(f32[64,512]{1,0:T(8,128)} %get-tuple-element.5) | copy-start | bytes 393220

commit v4 on v3

--- a/solution.py
+++ b/solution.py
@@ -32,11 +32,11 @@
 
 def kernel(
     n_leaf, n_loop, halves, x_hbm, l_hbm, u_hbm, v_hbm, c_hbm, g_hbm, order_ref,
-    cross_hbm, proj_hbm,
+    cross_hbm, proj_ref,
     x_ref, l_ref, u_ref, v_ref, c_ref, xp_ref, m_ref, mb_ref, n_ref, nrecv_ref,
     coef_ref, sums_ref, sib_ref, tot_ref, ends_ref, csend_ref, crecv_ref,
     w_ref, wrecv_ref, mixsend_ref, mixrecv_ref, mixall_ref,
-    f_ref, frecv_ref, zs_ref, zr_ref, red_ref, ag_ref, cross_ref, proj_ref,
+    f_ref, frecv_ref, zs_ref, zr_ref, red_ref, ag_ref, cross_ref,
     load_sem, store_sem, early_send, early_recv, chain_send, chain_recv,
     end_send, end_recv, mix_send, mix_recv, f_send, f_recv, z_send, z_recv,
     ag_send, ag_recv, wcat_ref, part_ref, qs_ref, qz_ref, q_send, q_recv,
@@ -244,34 +244,42 @@
         launch(pieces, 0, r)
 
     extra = pieces
-    for level in range(1, levels):
+
+    def receive(level, k):
+        for half in range(halves):
+            rows = rows_of(half)
+            chain[level, k, half].wait_recv()
+            tot_ref[level, k, rows] = tot_ref[level - 1, k, rows] + sums_ref[level - 1, k, rows]
+            if level + 1 < levels:
+                advance(level, k, half)
+            work(1)
+
+    def mixed(level, k):
+        both = jnp.concatenate([doubled(c_ref[level]), doubled(crecv_ref[level].astype(BF16))], axis=0)
+        return dot(both, stacked(sums_ref[level - 1, k]))
+
+    last = levels - 1
+    for level in range(1, last):
         for k in range(pieces):
-            for half in range(halves):
-                rows = rows_of(half)
-                chain[level, k, half].wait_recv()
-                tot_ref[level, k, rows] = tot_ref[level - 1, k, rows] + sums_ref[level - 1, k, rows]
-                if level + 1 < levels:
-                    advance(level, k, half)
-                work(1)
-        work(len(jobs))
-        if level == 1:
-            copy_n = send(
-                n_ref.at[pl.ds(other, pieces)], nrecv_ref,
-                early_send.at[pieces + 2], early_recv.at[pieces + 2], sibling, loop,
-            )
-
-    if chip_levels > 1:
-        collect(extra, 0)
-    own = [doubled(c_ref[b]) for b in range(levels)]
-    theirs = [doubled(crecv_ref[b].astype(BF16)) for b in range(levels)]
+            receive(level, k)
+    work(len(jobs))
+    copy_n = send(
+        n_ref.at[pl.ds(other, pieces)], nrecv_ref,
+        early_send.at[pieces + 2], early_recv.at[pieces + 2], sibling, loop,
+    )
     for k in range(pieces):
         value = jnp.concatenate([
-            dot(own[0], stacked(sib_ref[k])),
-            dot(theirs[0], stacked(coef_ref[mine + k])),
+            dot(doubled(c_ref[0]), stacked(sib_ref[k])),
+            dot(doubled(crecv_ref[0].astype(BF16)), stacked(coef_ref[mine + k])),
         ], axis=0)
-        for level in range(1, levels):
-            both = jnp.concatenate([own[level], theirs[level]], axis=0)
-            value = value + dot(both, stacked(sums_ref[level - 1, k]))
+        for level in range(1, last):
+            value = value + mixed(level, k)
+        part_ref[k] = value
+    for k in range(pieces):
+        if k == pieces - 1 and chip_levels > 1:
+            collect(extra, 0)
+        receive(last, k)
+        value = part_ref[k] + mixed(last, k)
         part_ref[k] = value
         rounded = value.astype(BF16)
         far = dot(wcat_ref[...], jnp.concatenate([rounded, rounded], axis=0))
@@ -391,8 +399,6 @@
                 left = (source * pieces + k) * width
                 proj_ref[at * z_rows:(at + 1) * z_rows, left:left + width] = ag_ref[source, at, k]
 
-    out_proj = pltpu.make_async_copy(proj_ref, proj_hbm, store_sem.at[1])
-    out_proj.start()
 
     for copy in first + [copy_c, copy_w, copy_n] + copy_q + mix_copies:
         copy.wait_send()
@@ -408,7 +414,6 @@
             gather(0, k).wait_send()
 
     out_cross.wait()
-    out_proj.wait()
 
 
 def solution(mesh):
@@ -436,7 +441,7 @@
                 jax.ShapeDtypeStruct((obs // n_leaf, obs), F32),
             ),
             in_specs=[anywhere] * 6 + [pl.BlockSpec(memory_space=pltpu.VMEM)],
-            out_specs=(anywhere, anywhere),
+            out_specs=(anywhere, pl.BlockSpec(memory_space=pltpu.VMEM)),
             scratch_shapes=[
                 vmem((cells, obs), BF16),
                 vmem((cells, cells), BF16),
@@ -467,7 +472,6 @@
                 vmem((pieces, z_rows, width), F32),
                 vmem((2, half_loop, pieces, z_rows, width), F32),
                 vmem((cells, obs), BF16),
-                vmem((obs // n_leaf, obs), F32),
                 dma((6,)),
                 dma((2,)),
                 dma((pieces + 3,)),

time: 38.5 us -> 41.3 us (1.073)
  Pallas kernels: 34.7 us -> 37.5 us
    pallas_call x1, Pallas kernels: 34.7 us -> 37.5 us  [body(): pl.pallas_call(functools.partial(kernel, n_leaf, n_loop, halves), out_sha...]
where the time goes in v4:
time: 41.3 us; the launch traced here: 41.1 us
  Pallas kernels  37.5 us (91%)
  local copies, waits for them, and re-layouts  2.96 us (7%)
  between operations  0.65 us (2%)
    pallas_call x1, Pallas kernels, body(): pl.pallas_call(functools.partial(kernel, n_leaf, n_loop, halves), out_sha...  37.5 us
    unnamed x4, local copies, waits for them, and re-layouts  2.96 us

profile of v4, /device:TPU:1, one launch (start us, length us, event | category | flops | bytes accessed | tf_op | source)
XLA Modules:
  0.0 41.1 jit_solution(5575102299236493239)
XLA Ops:
  0.6 37.5 %shard_map.86 = (bf16[1,1024,512]{2,1,0:T(8,128)(2,1)}, f32[64,512]{1,0:T(8,128)}) custom-call(bf16[1,1024,512]{2,1,0:T(8,128)(2,1)} %x_hbm.1, bf16[1,1024,1024]{2,1,0:T(8,128)(2,1)} %l_hbm.1, bf16[1,1024,128]{2,1,0:T(8,128)(2,1)} %u_hbm.1, bf16[1,1024,128]{2,1,0:T(8,128)(2,1)} %v_hbm.1, bf16[1,3,128,128]{3,2,1,0:T(8,128)(2,1)} %c_hbm.1, ...), custom_call_target="tpu_custom_call" | custom-call | tf_op jit(solution)/shard_map/pallas_call | solution.py:437
  38.2 0.0 copy-start
  38.2 2.3 %copy.11 = bf16[1,1024,512]{2,1,0:T(8,128)(2,1)} copy(bf16[1,1024,512]{2,1,0:T(8,128)(2,1)} %get-tuple-element.4) | data formatting | bytes 2097152
  40.5 0.0 copy-done
  40.5 0.7 %copy.12 = f32[64,512]{1,0:T(8,128)} copy(f32[64,512]{1,0:T(8,128)S(1)} %copy-done) | data formatting | bytes 262144
Async XLA Ops:
  38.2 2.3 %copy-start = (f32[64,512]{1,0:T(8,128)S(1)}, f32[64,512]{1,0:T(8,128)}, u32[]{:S(2)}) copy-start(f32[64,512]{1,0:T(8,128)} %get-tuple-element.5) | copy-start | bytes 393220
